TPU v7x, 512 devices: a whole 4x8x8 slice. The times are simulated.
512 devices in a mesh: energy: 128 (over z, y, core), transpor: 4 (over x).
Axes of the slice: x: 4, y: 8, z: 8, core: 2. Of those that a mesh axis runs over, the one named last changes fastest.
Arguments:
- onsite: float32 [4, 128, 128], P('transpor'), may hold values from -1 to 1, as said below
- hopping: float32 [4, 128, 128], P('transpor'), may hold values from -0.25 to 0.25
- selfenergy: float32 [128, 4, 128, 128], P('energy', 'transpor'), may hold values from -1 to 1, as said below
- broadening: float32 [128, 4, 128], P('energy', 'transpor'), may hold values from 0.1 to 0.5
Outputs:
- green: float32 [128, 2, 4, 128, 128], P('energy', None, 'transpor')
- polar: float32 [128, 2, 4, 128, 128], P('energy', None, 'transpor')
Inputs may be any that keep to these rules, and one draw needn't show every extreme that they name: `onsite`: each block is symmetric. `selfenergy`: each block is symmetric.
All inputs are finite; a program needn't handle non-finite values.
Results may differ from a plain program's by a relative error of at most 0.00021.
Values sent between devices are 32-bit elements; how exact they have to be, the bound alone decides.
A program may use at most 128 MiB of HBM per device.

v0:
```python
import math

import jax
import jax.numpy as jnp
from jax import lax
from jax.sharding import PartitionSpec as P

ENERGY_LOW = -1.5
ENERGY_HIGH = 1.5


def prefix_2(part, axis, combine, identity, reverse):
    count = lax.axis_size(axis)
    place = lax.axis_index(axis)
    ahead = count - 1 - place if reverse else place
    gathered = jax.tree.map(lambda a: lax.all_gather(a, axis), part)
    state = jax.tree.map(lambda a, e: jnp.zeros_like(a) + jnp.asarray(e, a.dtype), part, identity)

    def one(hop, state):
        source = count - 1 - hop if reverse else hop
        return combine(
            state, jax.tree.map(lambda a: lax.dynamic_index_in_dim(a, source, 0, False), gathered)
        )

    return lax.fori_loop(0, ahead, one, state)


def product(left, right):
    return jnp.matmul(left, right, precision=lax.Precision.HIGHEST)


def flipped(matrix):
    return jnp.swapaxes(matrix, -1, -2)


def complex_mul(first, second):
    return (
        product(first[0], second[0]) - product(first[1], second[1]),
        product(first[0], second[1]) + product(first[1], second[0]),
    )


def complex_add(first, second):
    return (first[0] + second[0], first[1] + second[1])


def complex_flip(value):
    return (flipped(value[0]), flipped(value[1]))


def real_left(matrix, value):
    return (product(matrix, value[0]), product(matrix, value[1]))


def real_right(value, matrix):
    return (product(value[0], matrix), product(value[1], matrix))


def invert(value):
    real_part, imag_part = value
    normal_real = product(flipped(real_part), real_part) + product(flipped(imag_part), imag_part)
    normal_imag = product(flipped(real_part), imag_part) - product(flipped(imag_part), real_part)
    upper_rows = jnp.concatenate([normal_real, -normal_imag], -1)
    lower_rows = jnp.concatenate([normal_imag, normal_real], -1)
    factor = jnp.linalg.cholesky(jnp.concatenate([upper_rows, lower_rows], -2))
    target = jnp.concatenate([flipped(real_part), -flipped(imag_part)], -2)
    solved = jax.scipy.linalg.cho_solve((factor, True), target)
    orders = real_part.shape[-1]
    return (solved[..., :orders, :], solved[..., orders:, :])


def joined(left, right, coupling):
    first_a, cross_a, last_a = left
    first_b, cross_b, last_b = right
    unit_matrix = jnp.eye(coupling.shape[-1], dtype=jnp.float32)
    dressing = real_right(real_left(coupling, first_b), flipped(coupling))
    loaded = complex_mul(last_a, dressing)
    kernel = invert((unit_matrix - loaded[0], -loaded[1]))
    weighted = complex_mul(kernel, last_a)
    first_new = complex_add(
        first_a,
        complex_mul(complex_mul(cross_a, complex_mul(dressing, kernel)), complex_flip(cross_a)),
    )
    bridge = real_left(coupling, cross_b)
    lifted = complex_add(cross_a, complex_mul(cross_a, complex_mul(dressing, weighted)))
    cross_new = complex_mul(lifted, bridge)
    last_new = complex_add(last_b, complex_mul(complex_flip(bridge), complex_mul(weighted, bridge)))
    return (first_new, cross_new, last_new)


def packed(corners, coupling, marker):
    return (
        corners[0][0],
        corners[0][1],
        corners[1][0],
        corners[1][1],
        corners[2][0],
        corners[2][1],
        coupling,
        marker,
    )


def unpacked(element):
    return ((element[0], element[1]), (element[2], element[3]), (element[4], element[5]))


def tree_join(earlier, later):
    merged = packed(
        joined(unpacked(earlier), unpacked(later), earlier[6]),
        later[6],
        jnp.maximum(earlier[7], later[7]),
    )
    has_early = earlier[7][0] > 0
    has_late = later[7][0] > 0
    return tuple(
        (
            jnp.where(has_early, jnp.where(has_late, whole_part, early_part), late_part)
            for whole_part, early_part, late_part in zip(merged, earlier, later)
        )
    )


def reverse_join(earlier, later):
    return tree_join(later, earlier)


def transform_sum(values):
    energy_total = values.shape[0]
    length = 2 * energy_total
    phase = (
        jnp.arange(length, dtype=jnp.int32)[:, None]
        * jnp.arange(energy_total, dtype=jnp.int32)[None, :]
        % length
    )
    angles = phase.astype(jnp.float32) * (2.0 * math.pi / length)
    cosine = jnp.cos(angles)
    sine_table = jnp.sin(angles)
    trailing = values.shape[2:]
    real_flat = values[:, 0].reshape(energy_total, -1)
    imag_flat = values[:, 1].reshape(energy_total, -1)
    spec_real = product(cosine, real_flat) + product(sine_table, imag_flat)
    spec_imag = product(cosine, imag_flat) - product(sine_table, real_flat)
    power = spec_real * spec_real + spec_imag * spec_imag
    real_sum = product(flipped(cosine), power) / (length * energy_total)
    imag_sum = product(flipped(sine_table), power) / (length * energy_total)
    return jnp.stack(
        [
            real_sum.reshape((energy_total,) + trailing),
            imag_sum.reshape((energy_total,) + trailing),
        ],
        1,
    )


def on_device(onsite, hopping, selfenergy, broadening):
    per_energy = selfenergy.shape[0]
    blocks = onsite.shape[0]
    orders = onsite.shape[-1]
    axis_span = lax.axis_size("transpor")
    energy_count = per_energy * lax.axis_size("energy")
    first_energy = lax.axis_index("energy") * per_energy
    levels = (
        ENERGY_LOW
        + (ENERGY_HIGH - ENERGY_LOW)
        * ((first_energy + jnp.arange(per_energy, dtype=jnp.int32)).astype(jnp.float32) + 0.5)
        / energy_count
    )
    unit_matrix = jnp.eye(orders, dtype=jnp.float32)
    outgoing = hopping[blocks - 1]
    at_end = (lax.axis_index("transpor") == axis_span - 1).astype(jnp.float32)
    contact = at_end * product(outgoing, flipped(outgoing))
    block_index = 0
    real_part = (
        levels[:, None, None] * unit_matrix - onsite[block_index] - selfenergy[:, block_index]
    )
    imag_part = broadening[:, block_index, :, None] * unit_matrix
    imag_part = imag_part + contact
    matrices = [(real_part, imag_part)]
    singles = [invert(matrix) for matrix in matrices]
    segment = (singles[0], singles[0], singles[0])
    element = packed(segment, outgoing, jnp.ones((1,), jnp.float32))
    neutral = tuple((jnp.zeros_like(member) for member in element))
    prefix = prefix_2(element, "transpor", tree_join, neutral, False)
    suffix = prefix_2(element, "transpor", reverse_join, neutral, True)
    sigma_left = real_right(real_left(flipped(prefix[6]), (prefix[4], prefix[5])), prefix[6])
    sigma_right = real_right(real_left(outgoing, (suffix[0], suffix[1])), flipped(outgoing))
    block_index = 0
    real_part, imag_part = matrices[block_index]
    real_part = real_part - sigma_left[0]
    imag_part = imag_part - sigma_left[1]
    real_part = real_part - sigma_right[0]
    imag_part = imag_part - sigma_right[1]
    connected = [invert((real_part, imag_part))]
    greens = [connected[-1]]
    green = jnp.stack(
        [
            jnp.stack([value_pair[0] for value_pair in greens], 1),
            jnp.stack([value_pair[1] for value_pair in greens], 1),
        ],
        1,
    )
    flattened = green.reshape(per_energy, 2, blocks, orders * orders)
    correlated = transform_sum(
        lax.all_to_all(flattened, "energy", split_axis=3, concat_axis=0, tiled=True)
    )
    returned = lax.all_to_all(correlated, "energy", split_axis=0, concat_axis=3, tiled=True)
    polar = returned.reshape(per_energy, 2, blocks, orders, orders)
    return (green, polar)


def solution(mesh):
    placed = (
        P("transpor", None, None),
        P("transpor", None, None),
        P("energy", "transpor", None, None),
        P("energy", "transpor", None),
    )
    return jax.shard_map(
        on_device,
        mesh=mesh,
        in_specs=placed,
        out_specs=(
            P("energy", None, "transpor", None, None),
            P("energy", None, "transpor", None, None),
        ),
        check_vma=False,
    )
```

profile of v0, /device:TPU:1, one launch (start us, length us, event | category | flops | bytes accessed | tf_op | source)
XLA Modules:
  0.0 622.7 jit_solution(16338300515268233573)
XLA Ops:
  5.0 11.7 %custom-call.41 = f32[1,128,128]{2,1,0:T(8,128)S(1)} custom-call(f32[1,128,128]{2,1,0:T(8,128)S(1)} %slice.245), custom_call_target="Cholesky" | custom-call | tf_op jit(solution)/shard_map/jit(cholesky)/cholesky/custom-call.2 | solution.py:65
  66.1 19.7 %custom-call.45 = f32[2,128,128]{1,2,0:T(8,128)S(1)} custom-call(f32[2,128,128]{2,1,0:T(8,128)S(1)} %get-tuple-element.401), custom_call_target="InvertDiagBlocksLowerTriangular" | custom-call | tf_op jit(solution)/shard_map/jit(_cho_solve)/triangular_solve/custom-call.4 | solution.py:67
  106.5 12.2 %while.64 = (s32[]{:T(128)}, f32[1,128,128]{2,1,0:T(8,128)S(1)}, f32[1,128,128]{2,1,0:T(8,128)S(1)}, f32[128,128]{1,0:T(8,128)S(1)}, f32[1]{0:T(128)}, /*index=5...) while((s32[]{:T(128)}, f32[1,128,128]{2,1,0:T(8,128)S(1)}, ...), condition=%wide.region_5.9_spmd, body=%wide.region_4.8_spmd.sunk | while | flops 806813952 | bytes 11471332 | solution.py:25
  119.3 214.8 %while.66 = (s32[]{:T(128)}, f32[1,128,128]{2,1,0:T(8,128)S(1)}, f32[1,128,128]{2,1,0:T(8,128)S(1)}, f32[1]{0:T(128)}, s32[]{:T(128)}, /*index=5*/f32[4,1]{0,1:T...) while((s32[]{:T(128)}, f32[1,128,128]{2,1,0:T(8,128)S(1)}, ...), condition=%wide.region_7.11_spmd, body=%wide.region_6.10_spmd.sunk | while | flops 806764800 | bytes 11342354 | solution.py:25
  122.9 11.7 %custom-call.68 = f32[1,128,128]{2,1,0:T(8,128)S(1)} custom-call(f32[1,128,128]{2,1,0:T(8,128)S(1)} %slice.430), custom_call_target="Cholesky" | custom-call | tf_op jit(solution)/shard_map/while/body/jit(cholesky)/cholesky/custom-call.2 | solution.py:65
  145.0 11.7 %custom-call.70 = f32[1,128,128]{2,1,0:T(8,128)S(1)} custom-call(f32[1,128,128]{2,1,0:T(8,128)S(1)} %fusion.661), custom_call_target="Cholesky" | custom-call | tf_op jit(solution)/shard_map/while/body/jit(cholesky)/cholesky/custom-call.3 | solution.py:65
  163.0 19.7 %custom-call.72 = f32[2,128,128]{1,2,0:T(8,128)S(1)} custom-call(f32[2,128,128]{2,1,0:T(8,128)S(1)} %get-tuple-element.889), custom_call_target="InvertDiagBlocksLowerTriangular" | custom-call | tf_op jit(solution)/shard_map/while/body/jit(_cho_solve)/triangular_solve/custom-call.4 | solution.py:67
  194.3 11.7 %custom-call.68 = f32[1,128,128]{2,1,0:T(8,128)S(1)} custom-call(f32[1,128,128]{2,1,0:T(8,128)S(1)} %slice.430), custom_call_target="Cholesky" | custom-call | tf_op jit(solution)/shard_map/while/body/jit(cholesky)/cholesky/custom-call.2 | solution.py:65
  216.5 11.7 %custom-call.70 = f32[1,128,128]{2,1,0:T(8,128)S(1)} custom-call(f32[1,128,128]{2,1,0:T(8,128)S(1)} %fusion.661), custom_call_target="Cholesky" | custom-call | tf_op jit(solution)/shard_map/while/body/jit(cholesky)/cholesky/custom-call.3 | solution.py:65
  234.4 19.7 %custom-call.72 = f32[2,128,128]{1,2,0:T(8,128)S(1)} custom-call(f32[2,128,128]{2,1,0:T(8,128)S(1)} %get-tuple-element.889), custom_call_target="InvertDiagBlocksLowerTriangular" | custom-call | tf_op jit(solution)/shard_map/while/body/jit(_cho_solve)/triangular_solve/custom-call.4 | solution.py:67
  265.8 11.7 %custom-call.68 = f32[1,128,128]{2,1,0:T(8,128)S(1)} custom-call(f32[1,128,128]{2,1,0:T(8,128)S(1)} %slice.430), custom_call_target="Cholesky" | custom-call | tf_op jit(solution)/shard_map/while/body/jit(cholesky)/cholesky/custom-call.2 | solution.py:65
  287.9 11.7 %custom-call.70 = f32[1,128,128]{2,1,0:T(8,128)S(1)} custom-call(f32[1,128,128]{2,1,0:T(8,128)S(1)} %fusion.661), custom_call_target="Cholesky" | custom-call | tf_op jit(solution)/shard_map/while/body/jit(cholesky)/cholesky/custom-call.3 | solution.py:65
  305.9 19.7 %custom-call.72 = f32[2,128,128]{1,2,0:T(8,128)S(1)} custom-call(f32[2,128,128]{2,1,0:T(8,128)S(1)} %get-tuple-element.889), custom_call_target="InvertDiagBlocksLowerTriangular" | custom-call | tf_op jit(solution)/shard_map/while/body/jit(_cho_solve)/triangular_solve/custom-call.4 | solution.py:67
  337.0 11.7 %custom-call.46 = f32[1,128,128]{2,1,0:T(8,128)S(1)} custom-call(f32[1,128,128]{2,1,0:T(8,128)S(1)} %slice.255), custom_call_target="Cholesky" | custom-call | tf_op jit(solution)/shard_map/jit(cholesky)/cholesky/custom-call.2 | solution.py:65
  359.3 11.7 %custom-call.48 = f32[1,128,128]{2,1,0:T(8,128)S(1)} custom-call(f32[1,128,128]{2,1,0:T(8,128)S(1)} %fusion.150), custom_call_target="Cholesky" | custom-call | tf_op jit(solution)/shard_map/jit(cholesky)/cholesky/custom-call.3 | solution.py:65
  378.1 19.7 %custom-call.50 = f32[2,128,128]{1,2,0:T(8,128)S(1)} custom-call(f32[2,128,128]{2,1,0:T(8,128)S(1)} %get-tuple-element.403), custom_call_target="InvertDiagBlocksLowerTriangular" | custom-call | tf_op jit(solution)/shard_map/jit(_cho_solve)/triangular_solve/custom-call.4 | solution.py:67
  399.4 12.1 %copy.118 = f32[1,1,1,16384]{1,2,0,3:T(1,128)} copy(f32[1,1,1,16384]{3,2,1,0:T(1,128)S(1)} %bitcast.935) | data formatting | bytes 131072 | tf_op jit(solution)/shard_map/stack | solution.py:196
  411.4 11.9 %copy.117 = f32[1,1,1,16384]{1,2,0,3:T(1,128)} copy(f32[1,1,1,16384]{3,2,1,0:T(1,128)S(1)} %bitcast.934) | data formatting | bytes 131072 | tf_op jit(solution)/shard_map/stack | solution.py:196
  423.4 20.7 %fusion.252 = f32[16384,1,1,2]{3,2,1,0:T(1,128)} fusion(f32[1,1,1,16384]{1,2,0,3:T(1,128)} %copy.118, f32[1,1,1,16384]{1,2,0,3:T(1,128)} %copy.117), kind=kLoop, calls=%fused_computation.405 | loop fusion | flops 32768 | bytes 262144
  444.6 74.5 %reduce.94 = f32[16384,2]{1,0:T(8,128)} reduce(f32[16384,1,1,2]{3,2,1,0:T(1,128)} %fusion.252, f32[]{:T(128)} %broadcast.260), dimensions={1,2}, to_apply=%fusion.252.reduce_sub_computation | reduce | bytes 262148
  526.6 40.4 %all_to_all.33 = f32[128,1,256]{2,1,0:T(1,128)S(1)} all-to-all(f32[128,1,256]{2,1,0:T(1,128)S(1)} %reshape.504), channel_id=1, replica_groups=mesh['energy'=128,'transpor'=4] {'energy'}, dimensions={0} | all-to-all | bytes 262144 | tf_op jit(solution)/shard_map/all_to_all | solution.py:205
  568.0 14.9 %reshape.505 = f32[16384,1,1,2]{3,2,1,0:T(1,128)} reshape(f32[128,256]{1,0:T(8,128)S(1)} %reduce.95) | data formatting | bytes 262144
  582.9 15.0 %copy.119 = f32[1,2,1,16384]{3,2,1,0:T(1,128)S(1)} copy(f32[1,2,1,16384]{1,2,0,3:T(1,128)} %bitcast.922) | data formatting | bytes 262144 | tf_op jit(solution)/shard_map/all_to_all | solution.py:205
  609.7 12.2 %all-to-all-done.1 = f32[128,2,1,128]{3,2,1,0:T(1,128)S(1)} async-done(((f32[128,2,1,128]{3,2,1,0:T(1,128)}), f32[128,2,1,128]{3,2,1,0:T(1,128)S(1)}, u32[]{:S(2)}, u32[]{:S(2)}) %all-to-all-start.1) | async-done | bytes 131104 | tf_op jit(solution)/shard_map/all_to_all | solution.py:207
  (290 shorter events, 210.3 us)
Async XLA Ops:
  119.3 214.8 %copy-start = (f32[1,128,128]{2,1,0:T(8,128)S(1)}, f32[1,128,128]{2,1,0:T(8,128)}, u32[]{:S(2)}) copy-start(f32[1,128,128]{2,1,0:T(8,128)} %param.14) | copy-start | bytes 196612
  603.4 18.4 %all-to-all-start.1 = ((f32[128,2,1,128]{3,2,1,0:T(1,128)}), f32[128,2,1,128]{3,2,1,0:T(1,128)S(1)}, u32[]{:S(2)}, u32[]{:S(2)}) async-start(f32[128,2,1,128]{3,2,1,0:T(1,128)} %copy.120), calls=%async_computation.1 | async-start | bytes 262144 | tf_op jit(solution)/shard_map/all_to_all | solution.py:207
where the time goes:
time: 630 us; the launch traced here: 623 us
  other arithmetic  368 us (58%)
  local copies, waits for them, and re-layouts  88.7 us (14%)
  blocking collectives  78.6 us (12%)
  matrix products  42 us (7%)
  loops' own time  23.3 us (4%)
  waiting for transfers between devices  12.2 us (2%)
    another operation x31, other arithmetic, invert(): factor = jnp.linalg.cholesky(jnp.concatenate([upper_rows, lower_rows], -2))  171 us
    another operation x17, other arithmetic, invert(): solved = jax.scipy.linalg.cho_solve((factor, True), target)  98.5 us
    unnamed x2, other arithmetic  95.1 us
    all_to_all x1, blocking collectives, on_device(): lax.all_to_all(flattened, 'energy', split_axis=3, concat_axis=0, tiled=True)  40.4 us
    dot_general x95, matrix products, product(): return jnp.matmul(left, right, precision=lax.Precision.HIGHEST)  31.8 us
    all_gather x3, blocking collectives, prefix_2(): gathered = jax.tree.map(lambda a: lax.all_gather(a, axis), part)  29.9 us
    unnamed x11, local copies, waits for them, and re-layouts  27.5 us
    another operation x2, local copies, waits for them, and re-layouts, on_device(): jnp.stack([jnp.stack([value_pair[0] for value_pair in greens], 1), jnp.st...  24 us
  transfers between devices with their start and end apart: 1, of which 1 were waited for; matrix products, arithmetic and copies ran while one was open for 0% of the time, Pallas kernels for 0%

commit v1 on v0

v1 whole, which is shorter than its diff:
```python
import jax
import jax.numpy as jnp
import numpy as np
from jax import lax
from jax.experimental import pallas as pl
from jax.experimental.pallas import tpu as pltpu
from jax.sharding import PartitionSpec as P

N = 128
NB = 8
NE = 128
ENERGY_LOW = -1.5
ENERGY_HIGH = 1.5
MESH = pl.DeviceIdType.MESH
HIGHEST = lax.Precision.HIGHEST
F32 = jnp.float32
BF16 = jnp.bfloat16


def correlation_tables():
    freq = np.arange(NE)[:, None]
    time = np.arange(NE)[None, :]
    angle = 2.0 * np.pi * ((freq * time) % (2 * NE)) / (2 * NE)
    cosine, sine = np.cos(angle), np.sin(angle)
    alternate = np.where(np.arange(NE) % 2 == 0, 1.0, -1.0)
    lower = sine.copy()
    lower[0] = alternate
    forward = np.concatenate([cosine, lower], 0)
    weight = np.full((NE,), 2.0)
    weight[0] = 1.0
    scale = 1.0 / (2 * NE * NE)
    upper_right = np.zeros((NE, NE))
    upper_right[:, 0] = alternate
    backward = scale * np.block([[cosine.T * weight[None, :], upper_right], [np.zeros((NE, NE)), 4.0 * sine.T]])

    def halves(table):
        high = table.astype(np.float32).astype(BF16)
        low = (table - high.astype(np.float64)).astype(np.float32).astype(BF16)
        return high, low

    fh, fl = halves(forward)
    bh, bl = halves(backward)
    return np.concatenate([fh, fh, fl], 1), np.concatenate([bh, bh, bl], 1)


def split2(x):
    high = x.astype(BF16)
    return high, (x - high.astype(F32)).astype(BF16)


def split3(x):
    high = x.astype(BF16).astype(F32)
    rest = x - high
    middle = rest.astype(BF16).astype(F32)
    return high, middle, rest - middle


def mm(a, b, dims=((1,), (0,))):
    return lax.dot_general(a, b, (dims, ((), ())), precision=HIGHEST, preferred_element_type=F32)


def lane_copy(x, column):
    return jnp.broadcast_to(x[:, column : column + 1], (NB, N))


def row_copy(x, row):
    return jnp.broadcast_to(x[row : row + 1, :], (NB, N))


def eliminate(pr, pi, lane, sub, first):
    columns = [(lane_copy(pr, first + j), lane_copy(pi, first + j)) for j in range(NB)]
    for row in range(NB):
        here = sub == row
        cr, ci = columns[row]
        dr, di = row_copy(cr, row), row_copy(ci, row)
        over = 1.0 / (dr * dr + di * di)
        ir, ni = dr * over, di * over
        fr = jnp.where(here, -ir, cr * ir + ci * ni)
        fi = jnp.where(here, ni, ci * ir - cr * ni)

        def step(xr, xi):
            rr, ri = row_copy(xr, row), row_copy(xi, row)
            return (
                jnp.where(here, 0.0, xr) - (fr * rr - fi * ri),
                jnp.where(here, 0.0, xi) - (fr * ri + fi * rr),
            )

        for j in range(row + 1, NB):
            columns[j] = step(*columns[j])
        hit = lane == first + row
        unit = jnp.where(here, 1.0, 0.0)
        pr, pi = step(jnp.where(hit, unit, pr), jnp.where(hit, 0.0, pi))
    return pr, pi


def rank_update(lr, li, wr, wi):
    ls = (split3(lr), split3(li))
    ws = (split3(wr), split3(wi))
    left, right = [], []
    for a, b in ((0, 0), (0, 1), (1, 0), (1, 1), (0, 2), (2, 0)):
        left += [ls[0][a], ls[1][a]]
        right += [
            jnp.concatenate([ws[0][b], ws[1][b]], 1),
            jnp.concatenate([-ws[1][b], ws[0][b]], 1),
        ]
    return lax.dot_general(
        jnp.concatenate(left, 0),
        jnp.concatenate(right, 0),
        (((0,), (0,)), ((), ())),
        precision=lax.Precision.DEFAULT,
        preferred_element_type=F32,
    )


def replace_rows(old, start, new):
    parts = [old[:start]] if start else []
    parts.append(new)
    if start + NB < N:
        parts.append(old[start + NB :])
    return jnp.concatenate(parts, 0)


def invert(mr, mi):
    lane = lax.broadcasted_iota(jnp.int32, (NB, N), 1)
    sub = lax.broadcasted_iota(jnp.int32, (NB, N), 0)
    pr, pi = mr[:NB], mi[:NB]
    for start in range(0, N, NB):
        wr, wi = eliminate(pr, pi, lane, sub, start)
        done = lane < start
        lr, li = jnp.where(done, -pr, pr), jnp.where(done, -pi, pi)
        if start + NB < N:
            active = (lane >= start) & (lane < start + NB)
            sr, si = mr[start + NB : start + 2 * NB], mi[start + NB : start + 2 * NB]
            pr, pi = jnp.where(active, 0.0, sr), jnp.where(active, 0.0, si)
            for j in range(NB):
                cr, ci = lane_copy(sr, start + j), lane_copy(si, start + j)
                xr, xi = row_copy(wr, j), row_copy(wi, j)
                pr = pr - (cr * xr - ci * xi)
                pi = pi - (cr * xi + ci * xr)
        update = rank_update(lr, li, jnp.where(lane == start + sub, wr + 1.0, wr), wi)
        mr = replace_rows(mr - update[:, :N], start, wr)
        mi = replace_rows(mi - update[:, N:], start, wi)
    return mr, mi


def fused(
    onsite,
    hopping,
    selfenergy,
    broadening,
    forward,
    backward,
    green,
    polar,
    real_in,
    side_in,
    diag_in,
    near,
    own,
    far,
    matrix,
    coupling,
    lifted,
    block,
    spread,
    sums,
    forward_table,
    backward_table,
    send_sem,
    recv_sem,
    far_sem,
    table_sem,
    swap_sem,
    green_sem,
    line_sem,
):
    x = lax.axis_index("transpor")
    e = lax.axis_index("energy")
    z, y, c = e // 16, lax.rem(e // 2, 8), lax.rem(e, 2)
    plane = z * 2 + c

    def plane_peer(s):
        i = lax.rem(plane + s, 16)
        return (i // 2) * 16 + y * 2 + lax.rem(i, 2)

    def row_peer(s):
        return z * 16 + lax.rem(y + s, 8) * 2 + c

    barrier = pltpu.get_barrier_semaphore()
    for s in range(1, 4):
        pl.semaphore_signal(barrier, inc=1, device_id={"transpor": lax.rem(x + s, 4)}, device_id_type=MESH)

    @pl.loop(1, 16)
    def _(s):
        pl.semaphore_signal(barrier, inc=1, device_id={"energy": plane_peer(s)}, device_id_type=MESH)

    @pl.loop(1, 8)
    def _(s):
        pl.semaphore_signal(barrier, inc=1, device_id={"energy": row_peer(s)}, device_id_type=MESH)

    tables = [
        pltpu.make_async_copy(forward, forward_table, table_sem.at[0]),
        pltpu.make_async_copy(backward, backward_table, table_sem.at[1]),
    ]
    for copy in tables:
        copy.start()

    level = ENERGY_LOW + (ENERGY_HIGH - ENERGY_LOW) * (e.astype(F32) + 0.5) / NE
    rows = lax.broadcasted_iota(jnp.int32, (N, N), 0)
    lanes = lax.broadcasted_iota(jnp.int32, (N, N), 1)
    unit = rows == lanes

    def diagonal(row):
        return jnp.where(unit, jnp.broadcast_to(row, (N, N)), 0.0)

    real_in[x] = jnp.where(unit, level, 0.0) - onsite[...] - selfenergy[...]
    diag_in[x] = jnp.broadcast_to(broadening[...], (8, N))

    @pl.when(x < 3)
    def _():
        side_in[x] = hopping[...]

    @pl.when(x == 3)
    def _():
        outgoing = hopping[...]
        side_in[x] = diagonal(broadening[...]) + mm(outgoing, outgoing, ((1,), (1,)))

    pl.semaphore_wait(barrier, 25)

    pieces = (real_in, side_in, diag_in)

    def copy_of(kind, source, target):
        ref = pieces[kind]
        return pltpu.make_async_remote_copy(
            src_ref=ref.at[source],
            dst_ref=ref.at[source],
            send_sem=send_sem.at[kind, target],
            recv_sem=recv_sem.at[kind, source],
            device_id={"transpor": target},
            device_id_type=MESH,
        )

    early = {0: [(0, 3), (2, 3), (0, 2), (2, 2)], 3: [(0, 0), (1, 0), (0, 1), (1, 1)]}
    later = {
        0: [(1, 3), (1, 2), (1, 1)],
        1: [(0, 2), (2, 2), (0, 3), (2, 3), (0, 0), (2, 0), (1, 0), (1, 2), (1, 3)],
        2: [(0, 1), (2, 1), (1, 1), (0, 0), (2, 0), (1, 0), (0, 3), (2, 3), (1, 3)],
    }
    for source, what in early.items():

        @pl.when(x == source)
        def _():
            for kind, target in what:
                copy_of(kind, source, target).start()

    right = x < 2

    @pl.when(right)
    def _():
        copy_of(0, 3, 0).wait_recv()
        copy_of(1, 3, 0).wait_recv()
        matrix[0] = real_in[3]
        matrix[1] = side_in[3]

    @pl.when(x >= 2)
    def _():
        copy_of(0, 0, 3).wait_recv()
        copy_of(2, 0, 3).wait_recv()
        matrix[0] = real_in[0]
        matrix[1] = diagonal(diag_in[0][:1])

    for source, what in later.items():

        @pl.when(x == source)
        def _():
            for kind, target in what:
                copy_of(kind, source, target).start()

    @pl.loop(1, 8)
    def _(s):
        pl.semaphore_signal(line_sem, inc=1, device_id={"energy": row_peer(s)}, device_id_type=MESH)

    far_copy = pltpu.make_async_remote_copy(
        src_ref=near,
        dst_ref=far,
        send_sem=far_sem.at[0],
        recv_sem=far_sem.at[1],
        device_id={"transpor": 3 - x},
        device_id_type=MESH,
    )

    def set_coupling(slot, plain, source):
        @pl.when(plain)
        def _():
            coupling[slot] = side_in[source]

        @pl.when(jnp.logical_not(plain))
        def _():
            coupling[slot] = side_in[source].T

    def dressed(slot, gr, gi):
        h = coupling[slot]
        half = mm(h, jnp.concatenate([gr, gi], 1))
        both = mm(jnp.concatenate([half[:, :N], half[:, N:]], 0), h, ((1,), (1,)))
        return half, both[:N], both[N:]

    def stage(number, carry):
        inverse_r, inverse_i = invert(matrix[0], matrix[1])

        @pl.when(number == 0)
        def _():
            near[0] = inverse_r
            near[1] = inverse_i
            far_copy.start()

            @pl.when(right)
            def _():
                copy_of(0, 2, 0).wait_recv()
                copy_of(2, 2, 0).wait_recv()
                copy_of(1, 2, 0).wait_recv()
                set_coupling(0, right, 2)
                matrix[0] = real_in[2]
                matrix[1] = diagonal(diag_in[2][:1])

            @pl.when(x >= 2)
            def _():
                copy_of(0, 1, 3).wait_recv()
                copy_of(2, 1, 3).wait_recv()
                copy_of(1, 0, 3).wait_recv()
                set_coupling(0, right, 0)
                matrix[0] = real_in[1]
                matrix[1] = diagonal(diag_in[1][:1])

            _, sr, si = dressed(0, inverse_r, inverse_i)
            matrix[0] = matrix[0] - sr
            matrix[1] = matrix[1] - si

        @pl.when(number == 1)
        def _():
            @pl.when(x == 0)
            def _():
                copy_of(0, 1, 0).wait_recv()
                copy_of(2, 1, 0).wait_recv()
                copy_of(1, 1, 0).wait_recv()

            @pl.when(x == 1)
            def _():
                copy_of(1, 0, 1).wait_recv()

            @pl.when(x == 2)
            def _():
                copy_of(1, 1, 2).wait_recv()

            @pl.when(x == 3)
            def _():
                copy_of(0, 2, 3).wait_recv()
                copy_of(2, 2, 3).wait_recv()
                copy_of(1, 1, 3).wait_recv()
                copy_of(1, 2, 3).wait_recv()

            set_coupling(1, right, 1)

            @pl.when(right)
            def _():
                set_coupling(2, x >= 2, 0)
                matrix[0] = real_in[1]
                matrix[1] = diagonal(diag_in[1][:1])

            @pl.when(x >= 2)
            def _():
                set_coupling(2, x >= 2, 2)
                matrix[0] = real_in[2]
                matrix[1] = diagonal(diag_in[2][:1])

            _, sr, si = dressed(1, inverse_r, inverse_i)
            far_copy.wait_recv()
            half, tr, ti = dressed(2, far[0], far[1])
            lifted[...] = half
            matrix[0] = matrix[0] - (sr + tr)
            matrix[1] = matrix[1] - (si + ti)

        @pl.when(number == 2)
        def _():
            @pl.when((x == 1) | (x == 2))
            def _():
                own[0] = inverse_r
                own[1] = inverse_i

            @pl.when((x == 0) | (x == 3))
            def _():
                half = lifted[...]
                ur, ui = half[:, :N], half[:, N:]
                first = mm(inverse_r, half)
                second = mm(inverse_i, half)
                vr = first[:, :N] - second[:, N:]
                vi = first[:, N:] + second[:, :N]
                v = jnp.concatenate([vr, vi], 1)
                first = mm(ur, v, ((0,), (0,)))
                second = mm(ui, v, ((0,), (0,)))
                own[0] = far[0] + (first[:, :N] - second[:, N:])
                own[1] = far[1] + (first[:, N:] + second[:, :N])

        return carry

    lax.fori_loop(0, 3, stage, 0)

    save = pltpu.make_async_copy(own, green, green_sem)
    save.start()
    pl.semaphore_wait(line_sem, 7)

    def exchange(source, target, slot):
        def copy(s):
            other = lax.rem(e + s, NE)
            return pltpu.make_async_remote_copy(
                src_ref=source.at[:, pl.ds(other, 1), :],
                dst_ref=target.at[:, pl.ds(e, 1), :],
                send_sem=swap_sem.at[slot, 0],
                recv_sem=swap_sem.at[slot, 1],
                device_id={"energy": other},
                device_id_type=MESH,
            )

        @pl.loop(1, NE)
        def _(s):
            copy(s).start()

        pltpu.make_async_copy(
            source.at[:, pl.ds(e, 1), :], target.at[:, pl.ds(e, 1), :], swap_sem.at[slot, 1]
        ).start()
        pltpu.make_async_copy(source, target, swap_sem.at[slot, 1]).wait()

    def sent(source, target, slot):
        part = pl.ds(0, NE - 1)
        pltpu.make_async_copy(source.at[:, part, :], target.at[:, part, :], swap_sem.at[slot, 0]).wait()

    exchange(own, spread, 0)
    for copy in tables:
        copy.wait()

    values = jnp.concatenate([spread[0], spread[1]], 1)
    high, low = split2(values)
    spec = jnp.dot(forward_table[...], jnp.concatenate([high, low, high], 0), preferred_element_type=F32)
    a, cc = spec[:NE, :N], spec[:NE, N:]
    d, b = spec[NE:, :N], spec[NE:, N:]
    first_row = lax.broadcasted_iota(jnp.int32, (NE, N), 0) == 0
    upper, lower = a * a + cc * cc, b * b + d * d
    power = jnp.concatenate(
        [jnp.where(first_row, upper, upper + lower), jnp.where(first_row, lower, a * b - cc * d)], 0
    )
    high, low = split2(power)
    both = jnp.dot(backward_table[...], jnp.concatenate([high, low, high], 0), preferred_element_type=F32)
    sums[0] = both[:NE]
    sums[1] = both[NE:]
    exchange(sums, block, 1)
    finish = pltpu.make_async_copy(block, polar, table_sem.at[0])
    finish.start()

    sent(own, spread, 0)
    sent(sums, block, 1)
    far_copy.wait_send()
    for source in range(4):

        @pl.when(x == source)
        def _():
            for kind, target in early.get(source, []) + later.get(source, []):
                copy_of(kind, source, target).wait_send()

    save.wait()
    finish.wait()


def on_device(onsite, hopping, selfenergy, broadening):
    forward, backward = correlation_tables()
    forward, backward = jnp.asarray(forward), jnp.asarray(backward)
    whole = pl.BlockSpec(memory_space=pltpu.VMEM)
    left = pl.BlockSpec(memory_space=pl.ANY)
    pair = jax.ShapeDtypeStruct((2, N, N), F32)
    green, polar = pl.pallas_call(
        fused,
        out_shape=(pair, pair),
        in_specs=[whole, whole, whole, whole, left, left],
        out_specs=(left, left),
        scratch_shapes=[
            pltpu.VMEM((4, N, N), F32),
            pltpu.VMEM((4, N, N), F32),
            pltpu.VMEM((4, 8, N), F32),
            pltpu.VMEM((2, N, N), F32),
            pltpu.VMEM((2, N, N), F32),
            pltpu.VMEM((2, N, N), F32),
            pltpu.VMEM((2, N, N), F32),
            pltpu.VMEM((3, N, N), F32),
            pltpu.VMEM((N, 2 * N), F32),
            pltpu.VMEM((2, N, N), F32),
            pltpu.VMEM((2, NE, N), F32),
            pltpu.VMEM((2, NE, N), F32),
            pltpu.VMEM(forward.shape, BF16),
            pltpu.VMEM(backward.shape, BF16),
            pltpu.SemaphoreType.DMA((3, 4)),
            pltpu.SemaphoreType.DMA((3, 4)),
            pltpu.SemaphoreType.DMA((2,)),
            pltpu.SemaphoreType.DMA((2,)),
            pltpu.SemaphoreType.DMA((2, 2)),
            pltpu.SemaphoreType.DMA,
            pltpu.SemaphoreType.REGULAR,
        ],
        compiler_params=pltpu.CompilerParams(
            collective_id=0, has_side_effects=True, vmem_limit_bytes=48 * 2**20
        ),
    )(onsite[0], hopping[0], selfenergy[0, 0], broadening[0], forward, backward)
    return green[None, :, None], polar[None, :, None]


def solution(mesh):
    placed = (
        P("transpor", None, None),
        P("transpor", None, None),
        P("energy", "transpor", None, None),
        P("energy", "transpor", None),
    )
    return jax.shard_map(
        on_device,
        mesh=mesh,
        in_specs=placed,
        out_specs=(
            P("energy", None, "transpor", None, None),
            P("energy", None, "transpor", None, None),
        ),
        check_vma=False,
    )
```

time: 630 us -> 64.8 us (0.10); the launches traced: 623 us -> 64.5 us
  other arithmetic: 368 us -> 0 us
  local copies, waits for them, and re-layouts: 88.7 us -> 6.4 us
  blocking collectives: 78.6 us -> 0 us
  Pallas kernels: 0 us -> 57.4 us
  matrix products: 42 us -> 0 us
  loops' own time: 23.3 us -> 0 us
  waiting for transfers between devices: 12.2 us -> 0 us
    another operation x50 -> x0, other arithmetic: 270 us -> none  [the longest x31 171 us: invert(): factor = jnp.linalg.cholesky(jnp.concatenate([upper_rows, lower_rows], -2))]
    unnamed x2 -> x0, other arithmetic: 95.1 us -> none
    pallas_call x0 -> x1, Pallas kernels: none -> 57.4 us  [on_device(): pl.pallas_call(fused, out_shape=(pair, pair), in_specs=[whole, whole, who...]
    another operation x58 -> x0, local copies, waits for them, and re-layouts: 45.5 us -> none  [the longest x2 24 us: on_device(): jnp.stack([jnp.stack([value_pair[0] for value_pair in greens], 1), jnp.st...]
    all_to_all x1 -> x0, blocking collectives: 40.4 us -> none  [on_device(): lax.all_to_all(flattened, 'energy', split_axis=3, concat_axis=0, tiled=True)]
    dot_general x95 -> x0, matrix products: 31.8 us -> none  [product(): return jnp.matmul(left, right, precision=lax.Precision.HIGHEST)]
    all_gather x3 -> x0, blocking collectives: 29.9 us -> none  [prefix_2(): gathered = jax.tree.map(lambda a: lax.all_gather(a, axis), part)]
    another operation x7 -> x0, loops' own time: 23.3 us -> none  [the longest x2 22.9 us: prefix_2(): return lax.fori_loop(0, ahead, one, state)]
  transfers between devices with their start and end apart: 1 -> 0, of which waited for: 1 -> 0; matrix products, arithmetic and copies ran while one was open for 0% -> 0% of each run, Pallas kernels for 0% -> 0%
where the time goes in v1:
time: 64.8 us; the launch traced here: 64.5 us
  Pallas kernels  57.4 us (89%)
  local copies, waits for them, and re-layouts  6.4 us (10%)
  between operations  0.65 us (1%)
    pallas_call x1, Pallas kernels, on_device(): pl.pallas_call(fused, out_shape=(pair, pair), in_specs=[whole, whole, who...  57.4 us
    unnamed x14, local copies, waits for them, and re-layouts  6.4 us

profile of v1, /device:TPU:1, one launch (start us, length us, event | category | flops | bytes accessed | tf_op | source)
XLA Modules:
  0.0 64.5 jit_solution(13107520860602461630)
XLA Ops:
  0.6 0.0 copy-start.5
  0.6 0.6 %copy-done.5 = f32[1,1,128]{2,1,0:T(1,128)S(1)} copy-done((f32[1,1,128]{2,1,0:T(1,128)S(1)}, f32[1,1,128]{2,1,0:T(1,128)}, u32[]{:S(2)}) %copy-start.5) | copy-done | bytes 536
  1.3 0.0 copy-start
  1.3 1.0 %copy-done = bf16[256,768]{1,0:T(8,128)(2,1)S(1)} copy-done((bf16[256,768]{1,0:T(8,128)(2,1)S(1)}, bf16[256,768]{1,0:T(8,128)(2,1)}, u32[]{:S(2)}) %copy-start) | copy-done | bytes 393240
  2.3 0.0 copy-start.1
  2.3 0.9 %copy-done.1 = bf16[256,384]{1,0:T(8,128)(2,1)S(1)} copy-done((bf16[256,384]{1,0:T(8,128)(2,1)S(1)}, bf16[256,384]{1,0:T(8,128)(2,1)}, u32[]{:S(2)}) %copy-start.1) | copy-done | bytes 196632
  3.2 0.0 copy-start.2
  3.2 0.8 %copy-done.2 = f32[1,128,128]{2,1,0:T(8,128)S(1)} copy-done((f32[1,128,128]{2,1,0:T(8,128)S(1)}, f32[1,128,128]{2,1,0:T(8,128)}, u32[]{:S(2)}) %copy-start.2) | copy-done | bytes 65560
  4.1 0.0 copy-start.3
  4.1 0.8 %copy-done.3 = f32[1,128,128]{2,1,0:T(8,128)S(1)} copy-done((f32[1,128,128]{2,1,0:T(8,128)S(1)}, f32[1,128,128]{2,1,0:T(8,128)}, u32[]{:S(2)}) %copy-start.3) | copy-done | bytes 65560
  4.9 0.0 copy-start.4
  4.9 0.8 %copy-done.4 = f32[1,1,128,128]{3,2,1,0:T(8,128)S(1)} copy-done((f32[1,1,128,128]{3,2,1,0:T(8,128)S(1)}, f32[1,1,128,128]{3,2,1,0:T(8,128)}, u32[]{:S(2)}) %copy-start.4) | copy-done | bytes 65560
  5.7 57.4 %shard_map.77 = (f32[2,128,128]{2,1,0:T(8,128)S(1)}, f32[2,128,128]{2,1,0:T(8,128)S(1)}) custom-call(f32[128,128]{1,0:T(8,128)S(1)} %bitcast.12, f32[128,128]{1,0:T(8,128)S(1)} %bitcast.13, f32[128,128]{1,0:T(8,128)S(1)} %bitcast.14, f32[1,128]{1,0:T(1,128)S(1)} %bitcast.15, bf16[256,384]{1,0:T(8,128)(2,1)S(1)} %copy-done.1, bf16[256,768]{1,0:T(8,128)(2,1)S(1)} %copy-done), custom_call_target="tpu_custom_call" | custom-call | tf_op jit(solution)/shard_map/pallas_call | solution.py:478
  63.1 0.7 %copy.12 = f32[1,2,1,128,128]{4,3,2,1,0:T(8,128)} copy(f32[1,2,1,128,128]{4,3,2,1,0:T(8,128)S(1)} %bitcast.11) | data formatting | bytes 262144
  63.8 0.7 %copy.13 = f32[1,2,1,128,128]{4,3,2,1,0:T(8,128)} copy(f32[1,2,1,128,128]{4,3,2,1,0:T(8,128)S(1)} %bitcast.10) | data formatting | bytes 262144
Async XLA Ops:
  0.6 0.7 %copy-start.5 = (f32[1,1,128]{2,1,0:T(1,128)S(1)}, f32[1,1,128]{2,1,0:T(1,128)}, u32[]{:S(2)}) copy-start(f32[1,1,128]{2,1,0:T(1,128)} %param.9) | copy-start | bytes 1540
  1.3 1.0 %copy-start = (bf16[256,768]{1,0:T(8,128)(2,1)S(1)}, bf16[256,768]{1,0:T(8,128)(2,1)}, u32[]{:S(2)}) copy-start(bf16[256,768]{1,0:T(8,128)(2,1)} %constant.5.clone.backward) | copy-start | bytes 1179652
  2.3 0.9 %copy-start.1 = (bf16[256,384]{1,0:T(8,128)(2,1)S(1)}, bf16[256,384]{1,0:T(8,128)(2,1)}, u32[]{:S(2)}) copy-start(bf16[256,384]{1,0:T(8,128)(2,1)} %constant.4.clone.forward) | copy-start | bytes 589828
  3.2 0.8 %copy-start.2 = (f32[1,128,128]{2,1,0:T(8,128)S(1)}, f32[1,128,128]{2,1,0:T(8,128)}, u32[]{:S(2)}) copy-start(f32[1,128,128]{2,1,0:T(8,128)} %param.6) | copy-start | bytes 196612
  4.1 0.8 %copy-start.3 = (f32[1,128,128]{2,1,0:T(8,128)S(1)}, f32[1,128,128]{2,1,0:T(8,128)}, u32[]{:S(2)}) copy-start(f32[1,128,128]{2,1,0:T(8,128)} %param.7) | copy-start | bytes 196612
  4.9 0.8 %copy-start.4 = (f32[1,1,128,128]{3,2,1,0:T(8,128)S(1)}, f32[1,1,128,128]{3,2,1,0:T(8,128)}, u32[]{:S(2)}) copy-start(f32[1,1,128,128]{3,2,1,0:T(8,128)} %param.8) | copy-start | bytes 196612

commit v2 on v1

v2 whole, which is shorter than its diff:
```python
import jax
import jax.numpy as jnp
import numpy as np
from jax import lax
from jax.experimental import pallas as pl
from jax.experimental.pallas import tpu as pltpu
from jax.sharding import PartitionSpec as P

N = 128
NB = 8
NE = 128
ENERGY_LOW = -1.5
ENERGY_HIGH = 1.5
MESH = pl.DeviceIdType.MESH
F32 = jnp.float32
BF16 = jnp.bfloat16


def correlation_tables():
    freq = np.arange(NE)[:, None]
    time = np.arange(NE)[None, :]
    angle = 2.0 * np.pi * ((freq * time) % (2 * NE)) / (2 * NE)
    cosine, sine = np.cos(angle), np.sin(angle)
    alternate = np.where(np.arange(NE) % 2 == 0, 1.0, -1.0)
    lower = sine.copy()
    lower[0] = alternate
    forward = np.concatenate([cosine, lower], 0)
    weight = np.full((NE,), 2.0)
    weight[0] = 1.0
    scale = 1.0 / (2 * NE * NE)
    upper_right = np.zeros((NE, NE))
    upper_right[:, 0] = alternate
    backward = scale * np.block([[cosine.T * weight[None, :], upper_right], [np.zeros((NE, NE)), 4.0 * sine.T]])

    def halves(table):
        high = table.astype(np.float32).astype(BF16)
        low = (table - high.astype(np.float64)).astype(np.float32).astype(BF16)
        return high, low

    fh, fl = halves(forward)
    bh, bl = halves(backward)
    return np.concatenate([fh, fh, fl], 1), np.concatenate([bh, bh, bl], 1)


def split2(x):
    high = x.astype(BF16)
    return high, (x - high.astype(F32)).astype(BF16)


def split3(x):
    high = x.astype(BF16).astype(F32)
    rest = x - high
    middle = rest.astype(BF16).astype(F32)
    return high, middle, rest - middle


def lane_copy(x, column):
    return jnp.take_along_axis(x, jnp.full((NB, N), column, jnp.int32), axis=1)


def row_copy(x, row):
    return jnp.broadcast_to(x[row : row + 1, :], (NB, N))


def product(a, b):
    return a[0] * b[0] - a[1] * b[1], a[0] * b[1] + a[1] * b[0]


def total(terms):
    while len(terms) > 1:
        odd = [terms[-1]] if len(terms) % 2 else []
        terms = [terms[i] + terms[i + 1] for i in range(0, len(terms) - 1, 2)] + odd
    return terms[0]


def eliminate(panel, sub, lane, units, first):
    columns = [(lane_copy(panel[0], first + j), lane_copy(panel[1], first + j)) for j in range(NB)]
    active = (lane >= first) & (lane < first + NB)
    unit = jnp.where(lane == first + sub, 1.0, 0.0)
    rest = (jnp.where(active, unit, panel[0]), jnp.where(active, 0.0, panel[1]))
    for row in range(NB):
        column = columns[row]
        pivot = (row_copy(column[0], row), row_copy(column[1], row))
        over = 1.0 / (pivot[0] * pivot[0] + pivot[1] * pivot[1])
        less = (column[0] - units[row], column[1])
        if row + 1 < NB:
            x = columns[row + 1]
            line = (row_copy(x[0], row), row_copy(x[1], row))
            line = (pivot[0] * line[0] + pivot[1] * line[1], pivot[0] * line[1] - pivot[1] * line[0])
            step = product(less, line)
            columns[row + 1] = (x[0] - step[0] * over, x[1] - step[1] * over)
        factor = (less[0] * pivot[0] + less[1] * pivot[1], less[1] * pivot[0] - less[0] * pivot[1])
        factor = (factor[0] * over, factor[1] * over)

        def reduced(x):
            step = product(factor, (row_copy(x[0], row), row_copy(x[1], row)))
            return x[0] - step[0], x[1] - step[1]

        for j in range(row + 2, NB):
            columns[j] = reduced(columns[j])
        rest = reduced(rest)
    return rest


def stacked(left, right):
    ls = (split3(left[0]), split3(left[1]))
    ws = (split3(right[0]), split3(right[1]))
    lhs, rhs = [], []
    for a, b in ((0, 0), (0, 1), (1, 0), (1, 1), (0, 2), (2, 0)):
        lhs += [ls[0][a], ls[1][a]]
        rhs += [
            jnp.concatenate([ws[0][b], ws[1][b]], 1),
            jnp.concatenate([-ws[1][b], ws[0][b]], 1),
        ]
    return jnp.concatenate(lhs, 0), jnp.concatenate(rhs, 0)


def invert(matrix):
    count = N // NB
    lane = lax.broadcasted_iota(jnp.int32, (NB, N), 1)
    sub = lax.broadcasted_iota(jnp.int32, (NB, N), 0)
    units = [jnp.where(sub == row, 1.0, 0.0) for row in range(NB)]
    tiles = [(matrix[0, NB * k : NB * k + NB, :], matrix[1, NB * k : NB * k + NB, :]) for k in range(count)]
    panel = tiles[0]
    for k in range(count):
        first = NB * k
        active = (lane >= first) & (lane < first + NB)
        solved = eliminate(panel, sub, lane, units, first)
        done = lane < first
        left = (jnp.where(done, -panel[0], panel[0]), jnp.where(done, -panel[1], panel[1]))
        tiles[k] = solved
        if k + 1 < count:
            below = tiles[k + 1]
            terms = []
            for row in range(NB):
                factor = (lane_copy(below[0], first + row), lane_copy(below[1], first + row))
                terms.append(product(factor, (row_copy(solved[0], row), row_copy(solved[1], row))))
            panel = (
                jnp.where(active, 0.0, below[0]) - total([t[0] for t in terms]),
                jnp.where(active, 0.0, below[1]) - total([t[1] for t in terms]),
            )
            tiles[k + 1] = panel
        order = list(range(k + 2, count)) + list(range(k))
        lhs, rhs = stacked(left, (jnp.where(lane == first + sub, solved[0] + 1.0, solved[0]), solved[1]))
        lhs = lhs.T
        lhs = jnp.concatenate([lhs[NB * i : NB * i + NB] for i in order], 0)
        update = lax.dot_general(
            lhs, rhs, (((1,), (0,)), ((), ())), precision=lax.Precision.DEFAULT, preferred_element_type=F32
        )
        for place, i in enumerate(order):
            rows = slice(NB * place, NB * place + NB)
            tiles[i] = (tiles[i][0] - update[rows, :N], tiles[i][1] - update[rows, N:])
    return jnp.concatenate([t[0] for t in tiles], 0), jnp.concatenate([t[1] for t in tiles], 0)


def left3(x):
    high, low = split2(x)
    return jnp.concatenate([high, high, low], 1)


def right3(x, axis=0):
    high, low = split2(x)
    return jnp.concatenate([high, low, high], axis)


def dot3(a, b, dims=((1,), (0,))):
    return lax.dot_general(a, b, (dims, ((), ())), preferred_element_type=F32)


def fused(
    onsite_in,
    hopping_in,
    selfenergy_in,
    broadening_in,
    forward,
    backward,
    own,
    polar,
    onsite,
    hopping,
    selfenergy,
    broadening,
    turned,
    real_in,
    side_in,
    diag_in,
    near,
    far,
    matrix,
    lifted,
    spread,
    sums,
    forward_table,
    backward_table,
    send_sem,
    recv_sem,
    far_sem,
    input_sem,
    swap_sem,
    line_sem,
):
    x = lax.axis_index("transpor")
    e = lax.axis_index("energy")
    z, y, c = e // 16, lax.rem(e // 2, 8), lax.rem(e, 2)
    plane = z * 2 + c

    def plane_peer(s):
        i = lax.rem(plane + s, 16)
        return (i // 2) * 16 + y * 2 + lax.rem(i, 2)

    def row_peer(s):
        return z * 16 + lax.rem(y + s, 8) * 2 + c

    inputs = [
        pltpu.make_async_copy(source, target, input_sem.at[i])
        for i, (source, target) in enumerate(
            (
                (onsite_in, onsite),
                (selfenergy_in, selfenergy),
                (broadening_in, broadening),
                (hopping_in, hopping),
                (forward, forward_table),
                (backward, backward_table),
            )
        )
    ]
    for copy in inputs[:4]:
        copy.start()

    barrier = pltpu.get_barrier_semaphore()
    for s in range(1, 4):
        pl.semaphore_signal(barrier, inc=1, device_id={"transpor": lax.rem(x + s, 4)}, device_id_type=MESH)

    @pl.loop(1, 16)
    def _(s):
        pl.semaphore_signal(barrier, inc=1, device_id={"energy": plane_peer(s)}, device_id_type=MESH)

    @pl.loop(1, 8)
    def _(s):
        pl.semaphore_signal(barrier, inc=1, device_id={"energy": row_peer(s)}, device_id_type=MESH)

    level = ENERGY_LOW + (ENERGY_HIGH - ENERGY_LOW) * (e.astype(F32) + 0.5) / NE
    rows = lax.broadcasted_iota(jnp.int32, (N, N), 0)
    lanes = lax.broadcasted_iota(jnp.int32, (N, N), 1)
    unit = rows == lanes

    def diagonal(row):
        return jnp.where(unit, jnp.broadcast_to(row, (N, N)), 0.0)

    for copy in inputs[:4]:
        copy.wait()
    real_in[x] = jnp.where(unit, level, 0.0) - onsite[...] - selfenergy[...]
    diag_in[x] = jnp.broadcast_to(broadening[...], (8, N))

    @pl.when(x == 0)
    def _():
        side_in[0] = hopping[...].T

    @pl.when(x == 1)
    def _():
        side_in[1] = hopping[...]
        turned[...] = hopping[...].T

    @pl.when(x == 2)
    def _():
        side_in[2] = hopping[...]

    @pl.when(x == 3)
    def _():
        outgoing = hopping[...]
        side_in[3] = diagonal(broadening[...]) + dot3(left3(outgoing), right3(outgoing, 1), ((1,), (1,)))

    pl.semaphore_wait(barrier, 25)

    pieces = (real_in, side_in, diag_in)

    def copy_of(kind, source, target):
        ref = pieces[kind]
        return pltpu.make_async_remote_copy(
            src_ref=turned if kind == 1 and source == 1 and target > 1 else ref.at[source],
            dst_ref=ref.at[source],
            send_sem=send_sem.at[kind, target],
            recv_sem=recv_sem.at[kind, source],
            device_id={"transpor": target},
            device_id_type=MESH,
        )

    early = {0: [(0, 0, 2), (2, 0, 2), (0, 0, 3), (2, 0, 3)], 3: [(0, 3, 1), (1, 3, 1), (0, 3, 0), (1, 3, 0)]}
    later = {
        0: [(1, 0, 2), (1, 0, 3), (1, 0, 1)],
        1: [(2, 1, 3), (0, 1, 3), (2, 1, 2), (0, 1, 2), (1, 1, 0), (2, 1, 0), (0, 1, 0), (1, 1, 3), (1, 1, 2)],
        2: [(2, 2, 0), (0, 2, 0), (1, 2, 0), (2, 2, 1), (0, 2, 1), (1, 2, 1), (2, 2, 3), (0, 2, 3), (1, 2, 3)],
    }
    for source, what in early.items():

        @pl.when(x == source)
        def _():
            for item in what:
                copy_of(*item).start()

    right = x < 2
    left = x >= 2

    @pl.when(right)
    def _():
        copy_of(0, 3, 0).wait_recv()
        copy_of(1, 3, 0).wait_recv()
        matrix[0] = real_in[3]
        matrix[1] = side_in[3]

    @pl.when(left)
    def _():
        copy_of(2, 0, 3).wait_recv()
        copy_of(0, 0, 3).wait_recv()
        matrix[0] = real_in[0]
        matrix[1] = diagonal(diag_in[0][:1])

    for source, what in later.items():

        @pl.when(x == source)
        def _():
            for item in what:
                copy_of(*item).start()

    @pl.loop(1, 8)
    def _(s):
        pl.semaphore_signal(line_sem, inc=1, device_id={"energy": row_peer(s)}, device_id_type=MESH)

    for copy in inputs[4:]:
        copy.start()

    far_copy = pltpu.make_async_remote_copy(
        src_ref=near,
        dst_ref=far,
        send_sem=far_sem.at[0],
        recv_sem=far_sem.at[1],
        device_id={"transpor": 3 - x},
        device_id_type=MESH,
    )

    def dressed(h, gr, gi):
        half = dot3(left3(h), right3(jnp.concatenate([gr, gi], 1)))
        both = dot3(left3(jnp.concatenate([half[:, :N], half[:, N:]], 0)), right3(h, 1), ((1,), (1,)))
        return half, both[:N], both[N:]

    def stage(number, carry):
        inverse_r, inverse_i = invert(matrix)

        @pl.when(number == 0)
        def _():
            near[0] = inverse_r
            near[1] = inverse_i
            far_copy.start()

            @pl.when(right)
            def _():
                copy_of(2, 2, 0).wait_recv()
                copy_of(0, 2, 0).wait_recv()
                copy_of(1, 2, 0).wait_recv()

            @pl.when(left)
            def _():
                copy_of(2, 1, 3).wait_recv()
                copy_of(0, 1, 3).wait_recv()
                copy_of(1, 0, 3).wait_recv()

            block = jnp.where(right, 2, 1)
            _, sr, si = dressed(side_in[jnp.where(right, 2, 0)], inverse_r, inverse_i)
            matrix[0] = real_in[block] - sr
            matrix[1] = diagonal(diag_in[block][:1]) - si

        @pl.when(number == 1)
        def _():
            @pl.when(x == 0)
            def _():
                copy_of(1, 1, 0).wait_recv()
                copy_of(2, 1, 0).wait_recv()
                copy_of(0, 1, 0).wait_recv()

            @pl.when(x == 1)
            def _():
                copy_of(1, 0, 1).wait_recv()

            @pl.when(x == 2)
            def _():
                copy_of(1, 1, 2).wait_recv()

            @pl.when(x == 3)
            def _():
                copy_of(1, 1, 3).wait_recv()
                copy_of(2, 2, 3).wait_recv()
                copy_of(0, 2, 3).wait_recv()
                copy_of(1, 2, 3).wait_recv()

            block = jnp.where(right, 1, 2)
            _, sr, si = dressed(side_in[1], inverse_r, inverse_i)
            far_copy.wait_recv()
            half, tr, ti = dressed(side_in[jnp.where(right, 0, 2)], far[0], far[1])
            lifted[...] = half
            matrix[0] = real_in[block] - (sr + tr)
            matrix[1] = diagonal(diag_in[block][:1]) - (si + ti)

        @pl.when(number == 2)
        def _():
            @pl.when((x == 1) | (x == 2))
            def _():
                own[0] = inverse_r
                own[1] = inverse_i

            @pl.when((x == 0) | (x == 3))
            def _():
                half = lifted[...]
                four = dot3(left3(jnp.concatenate([inverse_r, inverse_i], 0)), right3(half))
                v = jnp.concatenate([four[:N, :N] - four[N:, N:], four[:N, N:] + four[N:, :N]], 1)
                four = dot3(left3(half.T), right3(v))
                own[0] = far[0] + (four[:N, :N] - four[N:, N:])
                own[1] = far[1] + (four[:N, N:] + four[N:, :N])

        return carry

    lax.fori_loop(0, 3, stage, 0)

    pl.semaphore_wait(line_sem, 7)

    def ordered(i):
        odd = lax.rem(i, 2)
        return 4 + (1 - odd) * (i // 2) - odd * ((i + 1) // 2)

    def exchange(source, target, slot):
        def copy(s):
            oz = lax.rem(z + ordered(s // 16), 8)
            oy = lax.rem(y + ordered(lax.rem(s // 2, 8)), 8)
            other = oz * 16 + oy * 2 + lax.rem(c + 1 - lax.rem(s, 2), 2)
            return pltpu.make_async_remote_copy(
                src_ref=source.at[:, pl.ds(other, 1), :],
                dst_ref=target.at[:, pl.ds(e, 1), :],
                send_sem=swap_sem.at[slot, 0],
                recv_sem=swap_sem.at[slot, 1],
                device_id={"energy": other},
                device_id_type=MESH,
            )

        @pl.loop(0, NE - 1)
        def _(s):
            copy(s).start()

        pltpu.make_async_copy(
            source.at[:, pl.ds(e, 1), :], target.at[:, pl.ds(e, 1), :], swap_sem.at[slot, 1]
        ).start()
        pltpu.make_async_copy(source, target, swap_sem.at[slot, 1]).wait()

    def sent(source, target, slot):
        part = pl.ds(0, NE - 1)
        pltpu.make_async_copy(source.at[:, part, :], target.at[:, part, :], swap_sem.at[slot, 0]).wait()

    exchange(own, spread, 0)
    for copy in inputs[4:]:
        copy.wait()

    values = jnp.concatenate([spread[0], spread[1]], 1)
    spec = dot3(forward_table[...], right3(values))
    a, cc = spec[:NE, :N], spec[:NE, N:]
    d, b = spec[NE:, :N], spec[NE:, N:]
    first_row = lax.broadcasted_iota(jnp.int32, (NE, N), 0) == 0
    upper, lower = a * a + cc * cc, b * b + d * d
    power = jnp.concatenate(
        [jnp.where(first_row, upper, upper + lower), jnp.where(first_row, lower, a * b - cc * d)], 0
    )
    both = dot3(backward_table[...], right3(power))
    sums[0] = both[:NE]
    sums[1] = both[NE:]
    exchange(sums, polar, 1)

    sent(own, spread, 0)
    sent(sums, polar, 1)
    far_copy.wait_send()
    for source in range(4):

        @pl.when(x == source)
        def _():
            for item in early.get(source, []) + later.get(source, []):
                copy_of(*item).wait_send()


def on_device(onsite, hopping, selfenergy, broadening):
    forward, backward = correlation_tables()
    forward, backward = jnp.asarray(forward), jnp.asarray(backward)
    whole = pl.BlockSpec(memory_space=pltpu.VMEM)
    stay = pl.BlockSpec(memory_space=pltpu.HBM)
    pair = jax.ShapeDtypeStruct((2, N, N), F32)
    green, polar = pl.pallas_call(
        fused,
        out_shape=(pair, pair),
        in_specs=[stay] * 6,
        out_specs=(whole, whole),
        scratch_shapes=[
            pltpu.VMEM((N, N), F32),
            pltpu.VMEM((N, N), F32),
            pltpu.VMEM((N, N), F32),
            pltpu.VMEM((1, N), F32),
            pltpu.VMEM((N, N), F32),
            pltpu.VMEM((4, N, N), F32),
            pltpu.VMEM((4, N, N), F32),
            pltpu.VMEM((4, 8, N), F32),
            pltpu.VMEM((2, N, N), F32),
            pltpu.VMEM((2, N, N), F32),
            pltpu.VMEM((2, N, N), F32),
            pltpu.VMEM((N, 2 * N), F32),
            pltpu.VMEM((2, NE, N), F32),
            pltpu.VMEM((2, NE, N), F32),
            pltpu.VMEM(forward.shape, BF16),
            pltpu.VMEM(backward.shape, BF16),
            pltpu.SemaphoreType.DMA((3, 4)),
            pltpu.SemaphoreType.DMA((3, 4)),
            pltpu.SemaphoreType.DMA((2,)),
            pltpu.SemaphoreType.DMA((6,)),
            pltpu.SemaphoreType.DMA((2, 2)),
            pltpu.SemaphoreType.REGULAR,
        ],
        compiler_params=pltpu.CompilerParams(
            collective_id=0, has_side_effects=True, vmem_limit_bytes=48 * 2**20
        ),
    )(
        *(
            pltpu.with_memory_space_constraint(array, pltpu.HBM)
            for array in (onsite[0], hopping[0], selfenergy[0, 0], broadening[0], forward, backward)
        )
    )
    return green[None, :, None], polar[None, :, None]


def solution(mesh):
    placed = (
        P("transpor", None, None),
        P("transpor", None, None),
        P("energy", "transpor", None, None),
        P("energy", "transpor", None),
    )
    return jax.shard_map(
        on_device,
        mesh=mesh,
        in_specs=placed,
        out_specs=(
            P("energy", None, "transpor", None, None),
            P("energy", None, "transpor", None, None),
        ),
        check_vma=False,
    )
```

time: 64.8 us -> 58.4 us (0.901)
  local copies, waits for them, and re-layouts: 6.4 us -> 1.31 us
  Pallas kernels: 57.4 us -> 56.3 us
    unnamed x14 -> x2, local copies, waits for them, and re-layouts: 6.4 us -> 1.31 us
    pallas_call x1, Pallas kernels: 57.4 us -> 56.3 us  [on_device(): pl.pallas_call(fused, out_shape=(pair, pair), in_specs=[stay] * 6, out_sp...]
where the time goes in v2:
time: 58.4 us; the launch traced here: 58.2 us
  Pallas kernels  56.3 us (96%)
  local copies, waits for them, and re-layouts  1.31 us (2%)
  between operations  0.64 us (1%)
    pallas_call x1, Pallas kernels, on_device(): pl.pallas_call(fused, out_shape=(pair, pair), in_specs=[stay] * 6, out_sp...  56.3 us
    unnamed x2, local copies, waits for them, and re-layouts  1.31 us

profile of v2, /device:TPU:1, one launch (start us, length us, event | category | flops | bytes accessed | tf_op | source)
XLA Modules:
  0.0 58.2 jit_solution(3504002387242263652)
XLA Ops:
  0.6 56.3 %shard_map.77 = (f32[2,128,128]{2,1,0:T(8,128)S(1)}, f32[2,128,128]{2,1,0:T(8,128)S(1)}) custom-call(f32[128,128]{1,0:T(8,128)} %bitcast.12, f32[128,128]{1,0:T(8,128)} %bitcast.13, f32[128,128]{1,0:T(8,128)} %bitcast.14, f32[1,128]{1,0:T(1,128)} %bitcast.15, bf16[256,384]{1,0:T(8,128)(2,1)} %constant.4.clone.forward, bf16[256,768]{1,0:T(8,128)(2,1)} %constant.5.clone.backward), custom_call_target="tpu_custom_call" | custom-call | tf_op jit(solution)/shard_map/pallas_call | solution.py:491
  56.9 0.7 %copy.12 = f32[1,2,1,128,128]{4,3,2,1,0:T(8,128)} copy(f32[1,2,1,128,128]{4,3,2,1,0:T(8,128)S(1)} %bitcast.11) | data formatting | bytes 262144
  57.6 0.7 %copy.13 = f32[1,2,1,128,128]{4,3,2,1,0:T(8,128)} copy(f32[1,2,1,128,128]{4,3,2,1,0:T(8,128)S(1)} %bitcast.10) | data formatting | bytes 262144

commit v3 on v2

--- a/solution.py
+++ b/solution.py
@@ -422,28 +422,23 @@
 
     pl.semaphore_wait(line_sem, 7)
 
-    def ordered(i):
-        odd = lax.rem(i, 2)
-        return 4 + (1 - odd) * (i // 2) - odd * ((i + 1) // 2)
+    steps_z = [lax.rem(z + i, 8) * 16 for i in range(8)]
+    steps_y = [lax.rem(y + i, 8) * 2 for i in range(8)]
+    steps_c = [c, 1 - c]
+    order = [(i, j, k) for i in range(8) for j in range(8) for k in range(2)][1:]
+    order.sort(key=lambda o: -(min(o[0], 8 - o[0]) + min(o[1], 8 - o[1])))
 
     def exchange(source, target, slot):
-        def copy(s):
-            oz = lax.rem(z + ordered(s // 16), 8)
-            oy = lax.rem(y + ordered(lax.rem(s // 2, 8)), 8)
-            other = oz * 16 + oy * 2 + lax.rem(c + 1 - lax.rem(s, 2), 2)
-            return pltpu.make_async_remote_copy(
+        for i, j, k in order:
+            other = steps_z[i] + steps_y[j] + steps_c[k]
+            pltpu.make_async_remote_copy(
                 src_ref=source.at[:, pl.ds(other, 1), :],
                 dst_ref=target.at[:, pl.ds(e, 1), :],
                 send_sem=swap_sem.at[slot, 0],
                 recv_sem=swap_sem.at[slot, 1],
                 device_id={"energy": other},
                 device_id_type=MESH,
-            )
-
-        @pl.loop(0, NE - 1)
-        def _(s):
-            copy(s).start()
-
+            ).start()
         pltpu.make_async_copy(
             source.at[:, pl.ds(e, 1), :], target.at[:, pl.ds(e, 1), :], swap_sem.at[slot, 1]
         ).start()

time: 58.4 us -> 51.7 us (0.89)
  Pallas kernels: 56.3 us -> 49.6 us
    pallas_call x1, Pallas kernels: 56.3 us -> 49.6 us  [on_device(): pl.pallas_call(fused, out_shape=(pair, pair), in_specs=[stay] * 6, out_sp...]
where the time goes in v3:
time: 51.7 us; the launch traced here: 51.5 us
  Pallas kernels  49.6 us (96%)
  local copies, waits for them, and re-layouts  1.31 us (3%)
  between operations  0.64 us (1%)
    pallas_call x1, Pallas kernels, on_device(): pl.pallas_call(fused, out_shape=(pair, pair), in_specs=[stay] * 6, out_sp...  49.6 us
    unnamed x2, local copies, waits for them, and re-layouts  1.31 us

profile of v3, /device:TPU:1, one launch (start us, length us, event | category | flops | bytes accessed | tf_op | source)
XLA Modules:
  0.0 51.5 jit_solution(14382140950827282135)
XLA Ops:
  0.6 49.6 %shard_map.77 = (f32[2,128,128]{2,1,0:T(8,128)S(1)}, f32[2,128,128]{2,1,0:T(8,128)S(1)}) custom-call(f32[128,128]{1,0:T(8,128)} %bitcast.12, f32[128,128]{1,0:T(8,128)} %bitcast.13, f32[128,128]{1,0:T(8,128)} %bitcast.14, f32[1,128]{1,0:T(1,128)} %bitcast.15, bf16[256,384]{1,0:T(8,128)(2,1)} %constant.4.clone.forward, bf16[256,768]{1,0:T(8,128)(2,1)} %constant.5.clone.backward), custom_call_target="tpu_custom_call" | custom-call | tf_op jit(solution)/shard_map/pallas_call | solution.py:486
  50.2 0.7 %copy.12 = f32[1,2,1,128,128]{4,3,2,1,0:T(8,128)} copy(f32[1,2,1,128,128]{4,3,2,1,0:T(8,128)S(1)} %bitcast.11) | data formatting | bytes 262144
  50.9 0.7 %copy.13 = f32[1,2,1,128,128]{4,3,2,1,0:T(8,128)} copy(f32[1,2,1,128,128]{4,3,2,1,0:T(8,128)S(1)} %bitcast.10) | data formatting | bytes 262144

commit v4 on v3

--- a/solution.py
+++ b/solution.py
@@ -188,8 +188,10 @@
     far,
     matrix,
     lifted,
+    packed,
     spread,
     sums,
+    block,
     forward_table,
     backward_table,
     send_sem,
@@ -422,52 +424,187 @@
 
     pl.semaphore_wait(line_sem, 7)
 
-    steps_z = [lax.rem(z + i, 8) * 16 for i in range(8)]
-    steps_y = [lax.rem(y + i, 8) * 2 for i in range(8)]
-    steps_c = [c, 1 - c]
+    half = N // 2
+    tall = lax.broadcasted_iota(jnp.int32, (half, N), 0)
+    wide = lax.broadcasted_iota(jnp.int32, (half, N), 1)
+    low = wide < half
+    across = jnp.where(low, wide, wide - half)
+
+    def turn(v):
+        return pltpu.roll(v, half, 1)
+
+    top_r, top_i, end_r, end_i = own[0, :half], own[1, :half], own[0, half:], own[1, half:]
+    head = jnp.where(low, top_r, turn(top_i))
+    tail = jnp.where(low, turn(end_r), end_i)
+    packed[1] = jnp.where(low, turn(top_r), top_i)
+    packed[2] = jnp.where(across >= tall, head, tail)
+    middle = jnp.sum(jnp.where(across == tall, tail, 0.0), 0, keepdims=True)
+    packed[0, half - 8 :] = jnp.broadcast_to(middle, (8, N))
+
+    at_z = [lax.rem(z + i, 8) for i in range(8)]
+    at_y = [lax.rem(y + i, 8) * 2 for i in range(8)]
+    at_c = [c, 1 - c]
+    upper_z = [k // 4 for k in at_z]
+
+    def hops(o):
+        return min(o[0], 8 - o[0]) + min(o[1], 8 - o[1])
+
+    def rank(o):
+        return at_z[o[0]] * 16 + at_y[o[1]] + at_c[o[2]]
+
+    def row_of(o):
+        return lax.rem(at_z[o[0]], 4) * 16 + lax.rem(at_y[o[1]] + 8 * upper_z[o[0]], 16) + at_c[o[2]]
+
     order = [(i, j, k) for i in range(8) for j in range(8) for k in range(2)][1:]
-    order.sort(key=lambda o: -(min(o[0], 8 - o[0]) + min(o[1], 8 - o[1])))
-
-    def exchange(source, target, slot):
-        for i, j, k in order:
-            other = steps_z[i] + steps_y[j] + steps_c[k]
+    order.sort(key=lambda o: -hops(o))
+    mine = row_of((0, 0, 0))
+    last = half - 1
+    keepers = (3 * 16 + 7 * 2 + 1, 7 * 16 + 3 * 2 + 1)
+    keeps = (e == keepers[0]) | (e == keepers[1])
+
+    extras = [
+        pltpu.make_async_remote_copy(
+            src_ref=packed.at[0, pl.ds(last, 1), :],
+            dst_ref=spread.at[0, pl.ds(e, 1), :],
+            send_sem=swap_sem.at[2 + i, 0],
+            recv_sem=swap_sem.at[2, 1],
+            device_id={"energy": keeper},
+            device_id_type=MESH,
+        )
+        for i, keeper in enumerate(keepers)
+    ]
+    for extra, keeper in zip(extras, keepers):
+
+        @pl.when(e != keeper)
+        def _():
+            extra.start()
+
+    pair = pl.ds(1, 2)
+    for o in order:
+        pltpu.make_async_remote_copy(
+            src_ref=packed.at[pair, pl.ds(row_of(o), 1), :],
+            dst_ref=spread.at[pair, pl.ds(e, 1), :],
+            send_sem=swap_sem.at[0, 0],
+            recv_sem=swap_sem.at[0, 1],
+            device_id={"energy": rank(o)},
+            device_id_type=MESH,
+        ).start()
+    pltpu.make_async_copy(
+        packed.at[pair, pl.ds(mine, 1), :], spread.at[pair, pl.ds(e, 1), :], swap_sem.at[0, 1]
+    ).start()
+    pltpu.make_async_copy(sums.at[pair], spread.at[pair], swap_sem.at[0, 1]).wait()
+
+    @pl.when(keeps)
+    def _():
+        pltpu.make_async_copy(
+            packed.at[0, pl.ds(last, 1), :], spread.at[0, pl.ds(e, 1), :], swap_sem.at[2, 1]
+        ).start()
+        pltpu.make_async_copy(sums.at[0], spread.at[0], swap_sem.at[2, 1]).wait()
+
+    @pl.when(jnp.logical_not(keeps))
+    def _():
+        spread[0] = jnp.zeros((NE, N), F32)
+
+    for copy in inputs[4:]:
+        copy.wait()
+
+    values = jnp.concatenate([spread[0], spread[1], spread[2]], 1)
+    spec = dot3(forward_table[...], right3(values))
+    first_row = lax.broadcasted_iota(jnp.int32, (NE, N), 0) == 0
+    left_lanes = lax.broadcasted_iota(jnp.int32, (NE, N), 1) < half
+    powers = []
+    for part in range(3):
+        upper, lower = spec[:NE, N * part : N * part + N], spec[NE:, N * part : N * part + N]
+        square, lower_square = upper * upper, lower * lower
+        even = jnp.where(first_row, square, square + lower_square)
+        cross = upper * turn(lower)
+        odd = jnp.where(first_row, lower_square + turn(lower_square), cross - turn(cross))
+        powers.append(jnp.concatenate([even + turn(even), odd], 0))
+    both = dot3(backward_table[...], right3(jnp.concatenate(powers, 1)))
+    for part in range(3):
+        real, imag = both[:NE, N * part : N * part + N], both[NE:, N * part : N * part + N]
+        sums[part] = jnp.where(left_lanes, real, -imag)
+
+    def give(near_planes, tie_planes):
+        for o in order:
+            if hops(o) > 4:
+                continue
+            planes = near_planes if hops(o) < 4 else tie_planes
             pltpu.make_async_remote_copy(
-                src_ref=source.at[:, pl.ds(other, 1), :],
-                dst_ref=target.at[:, pl.ds(e, 1), :],
-                send_sem=swap_sem.at[slot, 0],
-                recv_sem=swap_sem.at[slot, 1],
-                device_id={"energy": other},
+                src_ref=sums.at[planes, pl.ds(rank(o), 1), :],
+                dst_ref=block.at[planes, pl.ds(mine, 1), :],
+                send_sem=swap_sem.at[1, 0] if hops(o) < 4 else swap_sem.at[3, 1],
+                recv_sem=swap_sem.at[1, 1],
+                device_id={"energy": rank(o)},
                 device_id_type=MESH,
             ).start()
         pltpu.make_async_copy(
-            source.at[:, pl.ds(e, 1), :], target.at[:, pl.ds(e, 1), :], swap_sem.at[slot, 1]
+            sums.at[near_planes, pl.ds(e, 1), :], block.at[near_planes, pl.ds(mine, 1), :], swap_sem.at[1, 1]
         ).start()
-        pltpu.make_async_copy(source, target, swap_sem.at[slot, 1]).wait()
-
-    def sent(source, target, slot):
-        part = pl.ds(0, NE - 1)
-        pltpu.make_async_copy(source.at[:, part, :], target.at[:, part, :], swap_sem.at[slot, 0]).wait()
-
-    exchange(own, spread, 0)
-    for copy in inputs[4:]:
-        copy.wait()
-
-    values = jnp.concatenate([spread[0], spread[1]], 1)
-    spec = dot3(forward_table[...], right3(values))
-    a, cc = spec[:NE, :N], spec[:NE, N:]
-    d, b = spec[NE:, :N], spec[NE:, N:]
-    first_row = lax.broadcasted_iota(jnp.int32, (NE, N), 0) == 0
-    upper, lower = a * a + cc * cc, b * b + d * d
-    power = jnp.concatenate(
-        [jnp.where(first_row, upper, upper + lower), jnp.where(first_row, lower, a * b - cc * d)], 0
-    )
-    both = dot3(backward_table[...], right3(power))
-    sums[0] = both[:NE]
-    sums[1] = both[NE:]
-    exchange(sums, polar, 1)
-
-    sent(own, spread, 0)
-    sent(sums, polar, 1)
+
+    @pl.when(jnp.logical_not(keeps))
+    def _():
+        give(pair, pl.ds(1 + upper_z[0], 1))
+
+    @pl.when(e == keepers[0])
+    def _():
+        give(pl.ds(0, 3), pl.ds(0, 2))
+
+    @pl.when(e == keepers[1])
+    def _():
+        give(pl.ds(0, 3), pl.ds(2, 1))
+
+    part = pl.ds(0, (2 * half + 1) // 3)
+    pltpu.make_async_copy(packed.at[:, part, :], block.at[:, part, :], swap_sem.at[1, 1]).wait()
+
+    corner, wedge = block[1], block[2]
+    middle = block[0, last:]
+    corner_t, wedge_t = corner.T, wedge.T
+    for part in range(2):
+        flat = wedge if part == 0 else turn(wedge)
+        side = turn(corner) if part == 0 else corner
+        line = jnp.broadcast_to(middle, (half, N))
+        line = line if part == 0 else turn(line)
+        mirror = wedge_t[half * part : half * part + half]
+        mirror = jnp.concatenate([mirror, mirror], 1)
+        under = corner_t[half * part : half * part + half]
+        under = jnp.concatenate([under, under], 1)
+        first = jnp.where(across >= tall, flat, mirror)
+        final = jnp.where(across < tall, flat, jnp.where(across > tall, mirror, line))
+        polar[part, :half] = jnp.where(low, first, side)
+        polar[part, half:] = jnp.where(low, under, turn(final))
+
+    for extra, keeper in zip(extras, keepers):
+
+        @pl.when(e != keeper)
+        def _():
+            extra.wait_send()
+
+    part = pl.ds(0, NE - 1)
+    pltpu.make_async_copy(sums.at[pair, part, :], spread.at[pair, part, :], swap_sem.at[0, 0]).wait()
+
+    near_part = pl.ds(0, sum(hops(o) < 4 for o in order))
+    tie_part = pl.ds(0, sum(hops(o) == 4 for o in order))
+
+    def given(near_count, tie_count):
+        for planes, part, sem in (
+            (pl.ds(0, near_count), near_part, swap_sem.at[1, 0]),
+            (pl.ds(0, tie_count), tie_part, swap_sem.at[3, 1]),
+        ):
+            pltpu.make_async_copy(sums.at[planes, part, :], spread.at[planes, part, :], sem).wait()
+
+    @pl.when(jnp.logical_not(keeps))
+    def _():
+        given(2, 1)
+
+    @pl.when(e == keepers[0])
+    def _():
+        given(3, 2)
+
+    @pl.when(e == keepers[1])
+    def _():
+        given(3, 1)
+
     far_copy.wait_send()
     for source in range(4):
 
@@ -501,15 +638,17 @@
             pltpu.VMEM((2, N, N), F32),
             pltpu.VMEM((2, N, N), F32),
             pltpu.VMEM((N, 2 * N), F32),
-            pltpu.VMEM((2, NE, N), F32),
-            pltpu.VMEM((2, NE, N), F32),
+            pltpu.VMEM((3, N // 2, N), F32),
+            pltpu.VMEM((3, NE, N), F32),
+            pltpu.VMEM((3, NE, N), F32),
+            pltpu.VMEM((3, N // 2, N), F32),
             pltpu.VMEM(forward.shape, BF16),
             pltpu.VMEM(backward.shape, BF16),
             pltpu.SemaphoreType.DMA((3, 4)),
             pltpu.SemaphoreType.DMA((3, 4)),
             pltpu.SemaphoreType.DMA((2,)),
             pltpu.SemaphoreType.DMA((6,)),
-            pltpu.SemaphoreType.DMA((2, 2)),
+            pltpu.SemaphoreType.DMA((4, 2)),
             pltpu.SemaphoreType.REGULAR,
         ],
         compiler_params=pltpu.CompilerParams(

time: 51.7 us -> 49.8 us (0.963)
  Pallas kernels: 49.6 us -> 47.7 us
    pallas_call x1, Pallas kernels: 49.6 us -> 47.7 us  [on_device(): pl.pallas_call(fused, out_shape=(pair, pair), in_specs=[stay] * 6, out_sp...]
where the time goes in v4:
time: 49.8 us; the launch traced here: 49.6 us
  Pallas kernels  47.7 us (96%)
  local copies, waits for them, and re-layouts  1.31 us (3%)
  between operations  0.64 us (1%)
    pallas_call x1, Pallas kernels, on_device(): pl.pallas_call(fused, out_shape=(pair, pair), in_specs=[stay] * 6, out_sp...  47.7 us
    unnamed x2, local copies, waits for them, and re-layouts  1.31 us

profile of v4, /device:TPU:1, one launch (start us, length us, event | category | flops | bytes accessed | tf_op | source)
XLA Modules:
  0.0 49.6 jit_solution(10752686581355209761)
XLA Ops:
  0.6 47.7 %shard_map.77 = (f32[2,128,128]{2,1,0:T(8,128)S(1)}, f32[2,128,128]{2,1,0:T(8,128)S(1)}) custom-call(f32[128,128]{1,0:T(8,128)} %bitcast.12, f32[128,128]{1,0:T(8,128)} %bitcast.13, f32[128,128]{1,0:T(8,128)} %bitcast.14, f32[1,128]{1,0:T(1,128)} %bitcast.15, bf16[256,384]{1,0:T(8,128)(2,1)} %constant.4.clone.forward, bf16[256,768]{1,0:T(8,128)(2,1)} %constant.5.clone.backward), custom_call_target="tpu_custom_call" | custom-call | tf_op jit(solution)/shard_map/pallas_call | solution.py:623
  48.3 0.7 %copy.12 = f32[1,2,1,128,128]{4,3,2,1,0:T(8,128)} copy(f32[1,2,1,128,128]{4,3,2,1,0:T(8,128)S(1)} %bitcast.11) | data formatting | bytes 262144
  49.0 0.7 %copy.13 = f32[1,2,1,128,128]{4,3,2,1,0:T(8,128)} copy(f32[1,2,1,128,128]{4,3,2,1,0:T(8,128)S(1)} %bitcast.10) | data formatting | bytes 262144
